TPU v7x, 512 devices: a whole 4x4x16 slice. The times are simulated.
512 devices in a mesh: band: 16 (over y_hi, x, core), tm: 32 (over y_lo, z).
Axes of the slice: x: 4, y: 4 (y_hi: 2, y_lo: 2; y = y_hi * 2 + y_lo), z: 16, core: 2. Of those that a mesh axis runs over, the one named last changes fastest.
Arguments:
- spectrum: bfloat16 [64, 128, 65536], P(None, 'band', 'tm'), may hold values from -6 to 6
- w_freq: bfloat16 [5, 64, 8], replicated, may hold values from -1 to 1
- b_freq: float32 [64], replicated, may hold values from -3 to 3
- dilation: int32 [64], replicated, may hold values from 1 to 128, as said below
- w_time: float32 [3, 64], replicated, may hold values from -3 to 3
- b_time: float32 [64], replicated, may hold values from -3 to 3
- w_mix: bfloat16 [128, 128], replicated, may hold values from -0.5 to 0.5
- ln_gain: float32 [64], replicated, may hold values from 0.1 to 1.9
- w_up: bfloat16 [64, 256], replicated, may hold values from -0.75 to 0.75
- b_up: float32 [256], replicated, may hold values from -3 to 3
- w_down: bfloat16 [256, 64], replicated, may hold values from -0.375 to 0.375
- b_down: float32 [64], replicated, may hold values from -3 to 3
- epoch_lengths: int32 [32, 8], P('tm'), may hold values from 1 to 1024, 2048 in all within a row
Outputs:
- epoch_mean: float32 [256, 8192], P('tm', 'band')
- epoch_power: float32 [256, 8192], P('tm', 'band')
Inputs may be any that keep to these rules, and one draw needn't show every extreme that they name: One channel has a dilation of exactly 128.
All inputs are finite; a program needn't handle non-finite values.
Results may differ from a plain program's by a relative error of at most 0.0015.
Values may be sent and summed in bfloat16 or wider, within the bound.
A program may use at most 64 MiB of HBM per device.

v0:
```python
import jax
import jax.numpy as jnp
from jax import lax
from jax.sharding import PartitionSpec as P


def padded_2(block, sides, width, periodic):
    for axis, dim in sides:
        count = lax.axis_size(axis)
        forward = [(i, i + 1) for i in range(count - 1)]
        if periodic:
            forward.append((count - 1, 0))
        backward = [(target, source) for source, target in forward]
        low = lax.ppermute(
            lax.slice_in_dim(block, block.shape[dim] - width, None, axis=dim), axis, forward
        )
        high = lax.ppermute(lax.slice_in_dim(block, 0, width, axis=dim), axis, backward)
        block = jnp.concatenate([low, block, high], axis=dim)
    return block


def dilated(ext, dilation, w_time, b_time, pad, length):

    def one(chan, step, taps, shift):
        left = lax.dynamic_slice_in_dim(chan, pad - step, length, 1).astype(jnp.float32)
        middle = chan[:, pad : pad + length].astype(jnp.float32)
        right = lax.dynamic_slice_in_dim(chan, pad + step, length, 1).astype(jnp.float32)
        return taps[0] * left + taps[1] * middle + taps[2] * right + shift

    return jax.vmap(one)(ext, dilation, w_time.T, b_time).astype(jnp.bfloat16)


def bin_filter(padded, w_freq, b_freq, bins):
    channels = w_freq.shape[1]
    group_size = w_freq.shape[2]
    tiled = jnp.tile(w_freq, (1, 1, channels // group_size))
    owner = jnp.arange(channels) // group_size
    keep = owner[:, None] == owner[None, :]
    blocks = jnp.where(keep[None], tiled, jnp.zeros_like(tiled))
    total = jnp.einsum(
        "co,cft->oft", blocks[0], padded[:, 0:bins], preferred_element_type=jnp.float32
    )
    for tap in range(1, w_freq.shape[0]):
        total = total + jnp.einsum(
            "co,cft->oft",
            blocks[tap],
            padded[:, tap : tap + bins],
            preferred_element_type=jnp.float32,
        )
    return jax.nn.gelu(total + b_freq[:, None, None], approximate=True).astype(jnp.bfloat16)


def on_device(
    spectrum,
    w_freq,
    b_freq,
    dilation,
    w_time,
    b_time,
    w_mix,
    ln_gain,
    w_up,
    b_up,
    w_down,
    b_down,
    epoch_lengths,
):
    channels = spectrum.shape[0]
    local_bins = spectrum.shape[1]
    block_frames = spectrum.shape[2]
    bands = lax.axis_size("band")
    piece = block_frames // bands
    all_bins = local_bins * bands
    padded = padded_2(spectrum, (("band", 1),), 2, False)
    spectral = bin_filter(padded, w_freq, b_freq, local_bins)
    swapped = lax.all_to_all(spectral, "band", split_axis=2, concat_axis=1, tiled=True)
    beside_all = padded_2(swapped, (("band", 2),), piece, True)
    outer_parts = jnp.concatenate([beside_all[:, :, 2 * piece :], beside_all[:, :, :piece]], axis=2)
    outer = padded_2(outer_parts, (("tm", 2),), piece, False)
    band_index = lax.axis_index("band")
    left = jnp.where(band_index == 0, outer[:, :, :piece], beside_all[:, :, :piece])
    right = jnp.where(
        band_index == bands - 1, outer[:, :, 3 * piece :], beside_all[:, :, 2 * piece :]
    )
    joined = jnp.concatenate([left, swapped, right], axis=2)
    filtered = dilated(joined, dilation, w_time, b_time, piece, piece)
    row = epoch_lengths[0]
    ends = jnp.cumsum(row)
    starts = ends - row
    frame_ids = lax.axis_index("band") * piece + jnp.arange(piece, dtype=jnp.int32)
    member = (
        (frame_ids[None, :] >= starts[:, None]) & (frame_ids[None, :] < ends[:, None])
    ).astype(jnp.float32)
    epochs_here = row.shape[0]
    bin_block = min(32, all_bins)

    def per_block(block_id):
        rows = lax.dynamic_slice_in_dim(w_mix, block_id * bin_block, bin_block, 0)
        mixed = jnp.einsum("gf,cfp->cgp", rows, filtered, preferred_element_type=jnp.float32)
        mean = jnp.mean(mixed, axis=0)
        var = jnp.mean((mixed - mean) ** 2, axis=0)
        normed = ((mixed - mean) * lax.rsqrt(var + 1e-05) * ln_gain[:, None, None]).astype(
            jnp.bfloat16
        )
        flat = normed.reshape(channels, bin_block * piece)
        hidden = (
            jnp.einsum("ch,cn->hn", w_up, flat, preferred_element_type=jnp.float32) + b_up[:, None]
        )
        hidden = jax.nn.gelu(hidden, approximate=True).astype(jnp.bfloat16)
        projected = (
            jnp.einsum("hc,hn->cn", w_down, hidden, preferred_element_type=jnp.float32)
            + b_down[:, None]
        )
        resid = lax.dynamic_slice_in_dim(filtered, block_id * bin_block, bin_block, 1).astype(
            jnp.float32
        )
        block_out = projected.reshape(channels, bin_block, piece) + resid
        sums = jnp.einsum("et,cft->efc", member, block_out, precision=lax.Precision.HIGHEST)
        squares = jnp.einsum(
            "et,cft->efc", member, block_out * block_out, precision=lax.Precision.HIGHEST
        )
        return (sums, squares)

    sums, squares = lax.map(per_block, jnp.arange(all_bins // bin_block, dtype=jnp.int32))
    sums = jnp.transpose(sums, (1, 0, 2, 3)).reshape(epochs_here, all_bins * channels)
    squares = jnp.transpose(squares, (1, 0, 2, 3)).reshape(epochs_here, all_bins * channels)
    total_sums, total_squares = (
        lax.psum_scatter(sums, "band", scatter_dimension=1, tiled=True),
        lax.psum_scatter(squares, "band", scatter_dimension=1, tiled=True),
    )
    lens = row.astype(jnp.float32)[:, None]
    return (total_sums / lens, total_squares / lens)


def solution(mesh):
    return jax.shard_map(
        on_device,
        mesh=mesh,
        in_specs=(
            P(None, "band", "tm"),
            P(),
            P(),
            P(),
            P(),
            P(),
            P(),
            P(),
            P(),
            P(),
            P(),
            P(),
            P("tm", None),
        ),
        out_specs=(P("tm", "band"), P("tm", "band")),
        check_vma=False,
    )
```

profile of v0, /device:TPU:2, one launch (start us, length us, event | category | flops | bytes accessed | tf_op | source)
XLA Modules:
  0.0 470.4 jit_solution(17832737130556438430)
XLA Ops:
  7.2 3.3 fusion.61
  10.7 1.9 collective-permute-start
  12.8 3.6 collective-permute-start.1
  16.6 2.8 fusion.54
  19.4 1.8 collective-permute-done
  21.2 1.2 constant_dynamic-update-slice_fusion
  22.5 0.7 fusion.50
  23.2 0.7 fusion.52
  23.9 0.7 fusion.48
  24.6 2.6 fusion.43
  27.3 4.3 copy.55
  31.6 6.3 %reshape.163 = bf16[16,2,32768]{2,1,0:T(2,128)(2,1)S(1)} reshape(bf16[2048,8,64]{2,1,0:T(8,128)(2,1)} %bitcast.139) | data formatting | bytes 4194304
  37.9 35.8 %all_to_all.18 = bf16[16,2,32768]{2,1,0:T(2,128)(2,1)} all-to-all(bf16[16,2,32768]{2,1,0:T(2,128)(2,1)S(1)} %reshape.163), channel_id=1, replica_groups=mesh['band'=16,'tm'=32] {'band'}, dimensions={0} | all-to-all | bytes 4194304 | tf_op jit(solution)/shard_map/all_to_all | solution.py:76
  73.7 7.4 %reshape.164 = bf16[2048,8,64]{2,1,0:T(8,128)(2,1)} reshape(bf16[16,2,32768]{2,1,0:T(2,128)(2,1)} %all_to_all.18) | data formatting | bytes 4194304
  81.1 6.9 %copy.57 = bf16[64,16,8,128]{3,2,1,0:T(8,128)(2,1)} copy(bf16[64,16,8,128]{0,2,3,1:T(8,128)(2,1)} %bitcast.140) | data formatting | bytes 4194304 | tf_op jit(solution)/shard_map/all_to_all | solution.py:76
  88.0 3.3 copy.58
  91.3 2.9 collective-permute-start.2
  94.2 3.4 collective-permute-start.4
  97.6 21.9 %collective-permute-done.2 = bf16[64,128,128]{1,0,2:T(8,128)(2,1)} collective-permute-done((bf16[64,128,128]{1,0,2:T(8,128)(2,1)S(1)}, bf16[64,128,128]{1,0,2:T(8,128)(2,1)}, u32[]{:S(2)}, u32[]{:S(2)}) %collective-permute-start.2) | collective-permute-done | bytes 2097184 | tf_op jit(solution)/shard_map/ppermute | solution.py:14
  119.5 5.3 %collective-permute-start.3 = (bf16[64,128,128]{1,0,2:T(8,128)(2,1)}, bf16[64,128,128]{1,0,2:T(8,128)(2,1)}, u32[]{:S(2)}, u32[]{:S(2)}) collective-permute-start(bf16[64,128,128]{1,0,2:T(8,128)(2,1)} %collective-permute-done.2), channel_id=1, source_target_pairs={{0,1},{1,2},{2,3},{3,4},{4,5},{5,6},{6,7},{7,8},{8,9},{9,10},{10,1... | collective-permute-start | bytes 6291464 | tf_op jit(solution)/shard_map/ppermute | solution.py:14
  124.9 1.3 collective-permute-start.5
  126.4 40.6 %collective-permute-done.3 = bf16[64,128,128]{1,0,2:T(8,128)(2,1)} collective-permute-done((bf16[64,128,128]{1,0,2:T(8,128)(2,1)}, bf16[64,128,128]{1,0,2:T(8,128)(2,1)}, u32[]{:S(2)}, u32[]{:S(2)}) %collective-permute-start.3) | collective-permute-done | bytes 2097184 | tf_op jit(solution)/shard_map/ppermute | solution.py:14
  167.0 1.8 broadcast_select_fusion.1
  168.9 3.6 collective-permute-done.5
  172.5 1.8 broadcast_select_fusion
  174.3 5.7 %pad_maximum_fusion = bf16[64,128,384]{1,0,2:T(8,128)(2,1)} fusion(bf16[64,128,128]{1,0,2:T(8,128)(2,1)S(1)} %broadcast_select_fusion, bf16[64,128,128]{1,0,2:T(8,128)(2,1)S(1)} %copy.58, bf16[64,128,128]{1,0,2:T(8,128)(2,1)S(1)} %broadcast_select_fusion.1), kind=kLoop, calls=%fused_computation.47 | loop fusion | flops 6291456 | bytes 12582912 | tf_op jit(solution)/shard_map/concatenate | solution.py:85
  180.0 9.8 %gather_fusion = bf16[64,128,128]{1,0,2:T(8,128)(2,1)} fusion(bf16[64,128,384]{1,0,2:T(8,128)(2,1)} %pad_maximum_fusion, s32[64]{0:T(128)S(1)} %get-tuple-element.195), kind=kCustom, calls=%fused_computation | custom fusion | bytes 4195072 | tf_op jit(solution)/shard_map/vmap()/gather | solution.py:25
  189.8 9.8 %gather_fusion.1 = bf16[64,128,128]{1,0,2:T(8,128)(2,1)} fusion(bf16[64,128,384]{1,0,2:T(8,128)(2,1)} %pad_maximum_fusion, s32[64]{0:T(128)S(1)} %get-tuple-element.196), kind=kCustom, calls=%fused_computation.1 | custom fusion | bytes 4195072 | tf_op jit(solution)/shard_map/vmap()/gather | solution.py:27
  199.6 5.2 %add_convert_fusion = bf16[64,128,128]{1,0,2:T(8,128)(2,1)} fusion(bf16[64,128,128]{1,0,2:T(8,128)(2,1)} %gather_fusion.1, bf16[64,128,128]{1,0,2:T(8,128)(2,1)S(1)} %copy.58, bf16[64,128,128]{1,0,2:T(8,128)(2,1)} %gather_fusion, f32[64]{0:T(128)S(1)} %copy-done.5, f32[64]{0:T(128)S(1)} %get-tuple-element.191, f32[64]{0:T(128)S(1)} %get-tuple-element.192, ...), kind=kLoop, calls=%fused_computation.57 | loop fusion | flops 10485760 | bytes 8389632 | tf_op jit(solution)/shard_map/convert_element_type | solution.py:30
  204.8 3.4 copy.62
  208.2 67.5 %while.13 = (s32[]{:T(128)}, f32[4,8,32,64]{2,1,3,0:T(8,128)}, f32[4,8,32,64]{2,1,3,0:T(8,128)}, s32[4]{0:T(128)S(1)}, bf16[128,128]{1,0:T(8,128)(2,1)}, /*index...) while((s32[]{:T(128)}, f32[4,8,32,64]{2,1,3,0:T(8,128)}, ...), condition=%wide.region_4.5_spmd.clone, body=%wide.region_1.4_spmd.clone.sunk | while | flops 399519744 | bytes 14905191 | solution.py:124
  208.5 0.6 dynamic_slice.25
  209.7 1.1 fusion.86
  211.0 1.0 multiply_convert_fusion.2
  212.0 3.1 fusion.87
  215.5 4.9 %fusion.89 = f32[4,8,32,64]{2,1,3,0:T(8,128)} fusion(f32[4,8,32,64]{2,1,3,0:T(8,128)} %get-tuple-element.306, s32[]{:T(128)} %get-tuple-element.304, f32[64,32,128]{2,1,0:T(8,128)S(1)} %bitcast_add_fusion.2, s32[128]{0:T(128)S(1)} %get-tuple-element.335, s32[8]{0:T(128)S(1)} %get-tuple-element.334, s32[8]{0:T(128)S(1)} %get-tuple-element.333), kind=kOutput, calls=%fused_computation.18.clone.1 | convolution fusion | flops 25432064 | bytes 1311808 | tf_op jit(solution)/shard_map/while/body/eval_jaxpr/et,cft->efc/dot_general | solution.py:119
  220.4 4.9 %fusion.88 = f32[4,8,32,64]{2,1,3,0:T(8,128)} fusion(f32[4,8,32,64]{2,1,3,0:T(8,128)} %get-tuple-element.305, s32[]{:T(128)} %get-tuple-element.304, f32[64,32,128]{2,1,0:T(8,128)S(1)} %bitcast_add_fusion.2, s32[128]{0:T(128)S(1)} %get-tuple-element.335, s32[8]{0:T(128)S(1)} %get-tuple-element.334, s32[8]{0:T(128)S(1)} %get-tuple-element.333), kind=kOutput, calls=%fused_computation.20.clone.1 | convolution fusion | flops 25169920 | bytes 1311808 | tf_op jit(solution)/shard_map/while/body/eval_jaxpr/et,cft->efc/dot_general | solution.py:118
  225.3 0.6 dynamic_slice.25
  226.5 1.1 fusion.86
  227.8 1.0 multiply_convert_fusion.2
  228.8 3.1 fusion.87
  232.3 4.9 %fusion.89 = f32[4,8,32,64]{2,1,3,0:T(8,128)} fusion(f32[4,8,32,64]{2,1,3,0:T(8,128)} %get-tuple-element.306, s32[]{:T(128)} %get-tuple-element.304, f32[64,32,128]{2,1,0:T(8,128)S(1)} %bitcast_add_fusion.2, s32[128]{0:T(128)S(1)} %get-tuple-element.335, s32[8]{0:T(128)S(1)} %get-tuple-element.334, s32[8]{0:T(128)S(1)} %get-tuple-element.333), kind=kOutput, calls=%fused_computation.18.clone.1 | convolution fusion | flops 25432064 | bytes 1311808 | tf_op jit(solution)/shard_map/while/body/eval_jaxpr/et,cft->efc/dot_general | solution.py:119
  237.2 4.9 %fusion.88 = f32[4,8,32,64]{2,1,3,0:T(8,128)} fusion(f32[4,8,32,64]{2,1,3,0:T(8,128)} %get-tuple-element.305, s32[]{:T(128)} %get-tuple-element.304, f32[64,32,128]{2,1,0:T(8,128)S(1)} %bitcast_add_fusion.2, s32[128]{0:T(128)S(1)} %get-tuple-element.335, s32[8]{0:T(128)S(1)} %get-tuple-element.334, s32[8]{0:T(128)S(1)} %get-tuple-element.333), kind=kOutput, calls=%fused_computation.20.clone.1 | convolution fusion | flops 25169920 | bytes 1311808 | tf_op jit(solution)/shard_map/while/body/eval_jaxpr/et,cft->efc/dot_general | solution.py:118
  242.1 0.6 dynamic_slice.25
  243.3 1.1 fusion.86
  244.7 1.0 multiply_convert_fusion.2
  245.6 3.1 fusion.87
  248.7 0.2 copy.83
  248.9 0.2 bitcast_add_fusion.2
  249.1 4.9 %fusion.89 = f32[4,8,32,64]{2,1,3,0:T(8,128)} fusion(f32[4,8,32,64]{2,1,3,0:T(8,128)} %get-tuple-element.306, s32[]{:T(128)} %get-tuple-element.304, f32[64,32,128]{2,1,0:T(8,128)S(1)} %bitcast_add_fusion.2, s32[128]{0:T(128)S(1)} %get-tuple-element.335, s32[8]{0:T(128)S(1)} %get-tuple-element.334, s32[8]{0:T(128)S(1)} %get-tuple-element.333), kind=kOutput, calls=%fused_computation.18.clone.1 | convolution fusion | flops 25432064 | bytes 1311808 | tf_op jit(solution)/shard_map/while/body/eval_jaxpr/et,cft->efc/dot_general | solution.py:119
  254.0 4.9 %fusion.88 = f32[4,8,32,64]{2,1,3,0:T(8,128)} fusion(f32[4,8,32,64]{2,1,3,0:T(8,128)} %get-tuple-element.305, s32[]{:T(128)} %get-tuple-element.304, f32[64,32,128]{2,1,0:T(8,128)S(1)} %bitcast_add_fusion.2, s32[128]{0:T(128)S(1)} %get-tuple-element.335, s32[8]{0:T(128)S(1)} %get-tuple-element.334, s32[8]{0:T(128)S(1)} %get-tuple-element.333), kind=kOutput, calls=%fused_computation.20.clone.1 | convolution fusion | flops 25169920 | bytes 1311808 | tf_op jit(solution)/shard_map/while/body/eval_jaxpr/et,cft->efc/dot_general | solution.py:118
  258.9 0.6 dynamic_slice.25
  260.2 1.1 fusion.86
  261.5 1.0 multiply_convert_fusion.2
  262.4 3.1 fusion.87
  265.9 4.9 %fusion.89 = f32[4,8,32,64]{2,1,3,0:T(8,128)} fusion(f32[4,8,32,64]{2,1,3,0:T(8,128)} %get-tuple-element.306, s32[]{:T(128)} %get-tuple-element.304, f32[64,32,128]{2,1,0:T(8,128)S(1)} %bitcast_add_fusion.2, s32[128]{0:T(128)S(1)} %get-tuple-element.335, s32[8]{0:T(128)S(1)} %get-tuple-element.334, s32[8]{0:T(128)S(1)} %get-tuple-element.333), kind=kOutput, calls=%fused_computation.18.clone.1 | convolution fusion | flops 25432064 | bytes 1311808 | tf_op jit(solution)/shard_map/while/body/eval_jaxpr/et,cft->efc/dot_general | solution.py:119
  270.8 4.9 %fusion.88 = f32[4,8,32,64]{2,1,3,0:T(8,128)} fusion(f32[4,8,32,64]{2,1,3,0:T(8,128)} %get-tuple-element.305, s32[]{:T(128)} %get-tuple-element.304, f32[64,32,128]{2,1,0:T(8,128)S(1)} %bitcast_add_fusion.2, s32[128]{0:T(128)S(1)} %get-tuple-element.335, s32[8]{0:T(128)S(1)} %get-tuple-element.334, s32[8]{0:T(128)S(1)} %get-tuple-element.333), kind=kOutput, calls=%fused_computation.20.clone.1 | convolution fusion | flops 25169920 | bytes 1311808 | tf_op jit(solution)/shard_map/while/body/eval_jaxpr/et,cft->efc/dot_general | solution.py:118
  275.7 1.5 copy.63
  277.3 0.9 reshape.130
  278.2 1.5 copy.64
  279.8 0.9 reshape.131
  280.7 89.1 %reduce-scatter.3.cloned.1.call-done = f32[8,512]{1,0:T(8,128)} async-done(((f32[8,8192]{1,0:T(8,128)}), f32[8,512]{1,0:T(8,128)}) %reduce-scatter.3.cloned.1.call-update) | async-done | bytes 16400 | tf_op jit(solution)/shard_map/reduce_scatter | solution.py:128
  369.8 92.3 %reduce-scatter.5.cloned.1.call-done = f32[8,512]{1,0:T(8,128)} async-done(((f32[8,8192]{1,0:T(8,128)}), f32[8,512]{1,0:T(8,128)}) %reduce-scatter.5.cloned.1.call-update) | async-done | bytes 16400 | tf_op jit(solution)/shard_map/reduce_scatter | solution.py:129
  462.2 1.4 broadcast_divide_fusion
  (64 shorter events, 2.7 us)
Async XLA Ops:
  7.2 9.4 %copy-start = (bf16[64,8,2048]{2,1,0:T(8,128)(2,1)S(1)}, bf16[64,8,2048]{2,1,0:T(8,128)(2,1)}, u32[]{:S(2)}) copy-start(bf16[64,8,2048]{2,1,0:T(8,128)(2,1)} %param.15) | copy-start | bytes 6291460
  7.2 9.4 %copy-start.2 = (bf16[5,64,8]{1,2,0:T(8,128)(2,1)S(1)}, bf16[5,64,8]{1,2,0:T(8,128)(2,1)}, u32[]{:S(2)}) copy-start(bf16[5,64,8]{1,2,0:T(8,128)(2,1)} %param.16) | copy-start | bytes 15364
  7.2 362.6 %reduce-scatter.3.cloned.1.call-start = ((), (), s32[]{:S(2)}) async-start(), calls=%async_computation.3 | async-start | bytes 278528 | tf_op jit(solution)/shard_map/reduce_scatter | solution.py:128
  10.7 10.5 %collective-permute-start = (bf16[64,2,2048]{2,0,1:T(8,128)(2,1)S(1)}, bf16[64,2,2048]{2,0,1:T(8,128)(2,1)S(1)}, u32[]{:S(2)}, u32[]{:S(2)}) collective-permute-start(bf16[64,2,2048]{2,0,1:T(8,128)(2,1)S(1)} %copy.79), channel_id=1, source_target_pairs={{0,32},{32,64},{64,96},{96,128},{128,160},{160,192},{192,224},{224... | collective-permute-start | bytes 1572872 | tf_op jit(solution)/shard_map/ppermute | solution.py:14
  12.8 11.1 %collective-permute-start.1 = (bf16[64,2,2048]{2,0,1:T(8,128)(2,1)S(1)}, bf16[64,2,2048]{2,0,1:T(8,128)(2,1)S(1)}, u32[]{:S(2)}, u32[]{:S(2)}) collective-permute-start(bf16[64,2,2048]{2,0,1:T(8,128)(2,1)S(1)} %copy.78), channel_id=1, source_target_pairs={{32,0},{64,32},{96,64},{128,96},{160,128},{192,160},{224,192},{256... | collective-permute-start | bytes 1572872 | tf_op jit(solution)/shard_map/ppermute | solution.py:17
  23.9 0.7 copy-start.4
  88.0 38.2 %copy-start.11 = (s32[1,8]{1,0:T(1,128)S(1)}, s32[1,8]{1,0:T(1,128)}, u32[]{:S(2)}) copy-start(s32[1,8]{1,0:T(1,128)} %param.27) | copy-start | bytes 100
  88.0 38.4 %copy-start.9 = (s32[64]{0:T(128)S(1)}, s32[64]{0:T(128)}, u32[]{:S(2)}) copy-start(s32[64]{0:T(128)} %param.18) | copy-start | bytes 772
  88.0 38.4 %copy-start.3 = (f32[3,64]{1,0:T(4,128)S(1)}, f32[3,64]{1,0:T(4,128)}, u32[]{:S(2)}) copy-start(f32[3,64]{1,0:T(4,128)} %param.19) | copy-start | bytes 2308
  91.3 28.2 %collective-permute-start.2 = (bf16[64,128,128]{1,0,2:T(8,128)(2,1)S(1)}, bf16[64,128,128]{1,0,2:T(8,128)(2,1)}, u32[]{:S(2)}, u32[]{:S(2)}) collective-permute-start(bf16[64,128,128]{1,0,2:T(8,128)(2,1)S(1)} %copy.58), channel_id=1, source_target_pairs={{0,32},{32,64},{64,96},{96,128},{128,160},{160,192},{192,224},{224... | collective-permute-start | bytes 6291464 | tf_op jit(solution)/shard_map/ppermute | solution.py:14
  94.2 30.6 %collective-permute-start.4 = (bf16[64,128,128]{1,0,2:T(8,128)(2,1)S(1)}, bf16[64,128,128]{1,0,2:T(8,128)(2,1)}, u32[]{:S(2)}, u32[]{:S(2)}) collective-permute-start(bf16[64,128,128]{1,0,2:T(8,128)(2,1)S(1)} %copy.58), channel_id=1, source_target_pairs={{32,0},{64,32},{96,64},{128,96},{160,128},{192,160},{224,192},{256... | collective-permute-start | bytes 6291464 | tf_op jit(solution)/shard_map/ppermute | solution.py:17
  119.5 47.5 %collective-permute-start.3 = (bf16[64,128,128]{1,0,2:T(8,128)(2,1)}, bf16[64,128,128]{1,0,2:T(8,128)(2,1)}, u32[]{:S(2)}, u32[]{:S(2)}) collective-permute-start(bf16[64,128,128]{1,0,2:T(8,128)(2,1)} %collective-permute-done.2), channel_id=1, source_target_pairs={{0,1},{1,2},{2,3},{3,4},{4,5},{5,6},{6,7},{7,8},{8,9},{9,10},{10,1... | collective-permute-start | bytes 6291464 | tf_op jit(solution)/shard_map/ppermute | solution.py:14
  124.9 47.6 %collective-permute-start.5 = (bf16[64,128,128]{1,0,2:T(8,128)(2,1)}, bf16[64,128,128]{1,0,2:T(8,128)(2,1)}, u32[]{:S(2)}, u32[]{:S(2)}) collective-permute-start(bf16[64,128,128]{1,0,2:T(8,128)(2,1)} %collective-permute-done.4), channel_id=1, source_target_pairs={{1,0},{2,1},{3,2},{4,3},{5,4},{6,5},{7,6},{8,7},{9,8},{10,9},{11,1... | collective-permute-start | bytes 6291464 | tf_op jit(solution)/shard_map/ppermute | solution.py:17
  189.8 9.8 %copy-start.5 = (f32[64]{0:T(128)S(1)}, f32[64]{0:T(128)}, u32[]{:S(2)}) copy-start(f32[64]{0:T(128)} %param.20) | copy-start | bytes 772
  204.8 3.4 copy-start.1
  204.8 3.4 copy-start.6
  204.8 3.4 copy-start.7
  204.8 3.4 copy-start.8
  204.8 3.4 copy-start.10
  278.2 184.0 %reduce-scatter.5.cloned.1.call-start = ((), (), s32[]{:S(2)}) async-start(), calls=%async_computation.4 | async-start | bytes 278528 | tf_op jit(solution)/shard_map/reduce_scatter | solution.py:129
Sparse Core Ops, SparseCore 0:
  278.3 91.4 reduce-scatter.2
  374.4 87.6 reduce-scatter.4
where the time goes:
time: 472 us; the launch traced here: 470 us
  waiting for transfers between devices  249 us (53%)
  local copies, waits for them, and re-layouts  64.1 us (14%)
  matrix products  63.5 us (13%)
  blocking collectives  35.8 us (8%)
  other arithmetic  21.6 us (5%)
  starting transfers between devices  18.6 us (4%)
  between operations  14.4 us (3%)
    reduce_scatter x1, waiting for transfers between devices, on_device(): lax.psum_scatter(squares, 'band', scatter_dimension=1, tiled=True)  92.3 us
    reduce_scatter x1, waiting for transfers between devices, on_device(): lax.psum_scatter(sums, 'band', scatter_dimension=1, tiled=True)  89.1 us
    ppermute x3, waiting for transfers between devices, padded_2(): lax.ppermute(lax.slice_in_dim(block, block.shape[dim] - width, None, axis...  64.3 us
    all_to_all x1, blocking collectives, on_device(): lax.all_to_all(spectral, 'band', split_axis=2, concat_axis=1, tiled=True)  35.8 us
    dot_general x4, matrix products, per_block(): jnp.einsum('et,cft->efc', member, block_out, precision=lax.Precision.HIGH...  19.6 us
    dot_general x4, matrix products, per_block(): jnp.einsum('et,cft->efc', member, block_out * block_out, precision=lax.Pr...  19.6 us
    unnamed x30, local copies, waits for them, and re-layouts  17.5 us
    dot_general x4, matrix products, per_block(): jnp.einsum('hc,hn->cn', w_down, hidden, preferred_element_type=jnp.float32)  12.4 us
  transfers between devices with their start and end apart: 8, of which 6 were waited for; matrix products, arithmetic and copies ran while one was open for 2% of the time, Pallas kernels for 0%

commit v1 on v0

--- a/solution.py
+++ b/solution.py
@@ -73,7 +73,10 @@
     all_bins = local_bins * bands
     padded = padded_2(spectrum, (("band", 1),), 2, False)
     spectral = bin_filter(padded, w_freq, b_freq, local_bins)
-    swapped = lax.all_to_all(spectral, "band", split_axis=2, concat_axis=1, tiled=True)
+    devices = lax.axis_size("band")
+    shards = jnp.stack(jnp.split(spectral, devices, axis=2), axis=0)
+    shards = lax.all_to_all(shards, "band", split_axis=0, concat_axis=0)
+    swapped = jnp.concatenate(shards, axis=1)
     beside_all = padded_2(swapped, (("band", 2),), piece, True)
     outer_parts = jnp.concatenate([beside_all[:, :, 2 * piece :], beside_all[:, :, :piece]], axis=2)
     outer = padded_2(outer_parts, (("tm", 2),), piece, False)

time: 472 us -> 448 us (0.949)
  local copies, waits for them, and re-layouts: 64.1 us -> 40.5 us
    unnamed x30 -> x43, local copies, waits for them, and re-layouts: 17.5 us -> 4.51 us
    all_to_all x2 -> x0, local copies, waits for them, and re-layouts: 10.2 us -> none  [on_device(): lax.all_to_all(spectral, 'band', split_axis=2, concat_axis=1, tiled=True)]
where the time goes in v1:
time: 448 us; the launch traced here: 447 us
  waiting for transfers between devices  249 us (56%)
  matrix products  63.5 us (14%)
  local copies, waits for them, and re-layouts  40.5 us (9%)
  blocking collectives  35.8 us (8%)
  other arithmetic  21.6 us (5%)
  starting transfers between devices  18.6 us (4%)
  between operations  14.4 us (3%)
    reduce_scatter x1, waiting for transfers between devices, on_device(): lax.psum_scatter(squares, 'band', scatter_dimension=1, tiled=True)  92.3 us
    reduce_scatter x1, waiting for transfers between devices, on_device(): lax.psum_scatter(sums, 'band', scatter_dimension=1, tiled=True)  89.1 us
    ppermute x3, waiting for transfers between devices, padded_2(): lax.ppermute(lax.slice_in_dim(block, block.shape[dim] - width, None, axis...  64.1 us
    all_to_all x1, blocking collectives, on_device(): shards = lax.all_to_all(shards, 'band', split_axis=0, concat_axis=0)  35.8 us
    dot_general x4, matrix products, per_block(): jnp.einsum('et,cft->efc', member, block_out, precision=lax.Precision.HIGH...  19.6 us
    dot_general x4, matrix products, per_block(): jnp.einsum('et,cft->efc', member, block_out * block_out, precision=lax.Pr...  19.6 us
    dot_general x4, matrix products, per_block(): jnp.einsum('hc,hn->cn', w_down, hidden, preferred_element_type=jnp.float32)  12.4 us
    ppermute x3, starting transfers between devices, padded_2(): lax.ppermute(lax.slice_in_dim(block, block.shape[dim] - width, None, axis...  10 us
  transfers between devices with their start and end apart: 8, of which 6 were waited for; matrix products, arithmetic and copies ran while one was open for 2% of the time, Pallas kernels for 0%

profile of v1, /device:TPU:2, one launch (start us, length us, event | category | flops | bytes accessed | tf_op | source)
XLA Modules:
  0.0 446.7 jit_solution(14770787725092758281)
XLA Ops:
  7.2 3.3 fusion.77
  10.7 1.9 collective-permute-start
  12.8 3.6 collective-permute-start.1
  16.6 2.8 fusion.70
  19.4 1.8 collective-permute-done
  21.2 1.2 constant_dynamic-update-slice_fusion
  22.5 0.7 fusion.50
  23.2 0.7 fusion.52
  23.9 0.7 fusion.48
  24.6 2.6 fusion.43
  28.1 35.8 %all_to_all.5 = bf16[16,64,8,128]{3,1,2,0:T(8,128)(2,1)} all-to-all(bf16[16,64,8,128]{3,1,2,0:T(8,128)(2,1)S(1)} %fusion.54), channel_id=1, replica_groups=mesh['band'=16,'tm'=32] {'band'}, dimensions={0} | all-to-all | bytes 4194304 | tf_op jit(solution)/shard_map/all_to_all | solution.py:78
  63.9 3.9 copy.20
  67.8 2.9 collective-permute-start.2
  70.7 3.4 collective-permute-start.4
  74.1 21.9 %collective-permute-done.2 = bf16[64,128,128]{1,0,2:T(8,128)(2,1)} collective-permute-done((bf16[64,128,128]{1,0,2:T(8,128)(2,1)S(1)}, bf16[64,128,128]{1,0,2:T(8,128)(2,1)}, u32[]{:S(2)}, u32[]{:S(2)}) %collective-permute-start.2) | collective-permute-done | bytes 2097184 | tf_op jit(solution)/shard_map/ppermute | solution.py:14
  96.0 5.2 %collective-permute-start.3 = (bf16[64,128,128]{1,0,2:T(8,128)(2,1)}, bf16[64,128,128]{1,0,2:T(8,128)(2,1)}, u32[]{:S(2)}, u32[]{:S(2)}) collective-permute-start(bf16[64,128,128]{1,0,2:T(8,128)(2,1)} %collective-permute-done.2), channel_id=1, source_target_pairs={{0,1},{1,2},{2,3},{3,4},{4,5},{5,6},{6,7},{7,8},{8,9},{9,10},{10,1... | collective-permute-start | bytes 6291464 | tf_op jit(solution)/shard_map/ppermute | solution.py:14
  101.2 1.5 collective-permute-start.5
  102.9 40.4 %collective-permute-done.3 = bf16[64,128,128]{1,0,2:T(8,128)(2,1)} collective-permute-done((bf16[64,128,128]{1,0,2:T(8,128)(2,1)}, bf16[64,128,128]{1,0,2:T(8,128)(2,1)}, u32[]{:S(2)}, u32[]{:S(2)}) %collective-permute-start.3) | collective-permute-done | bytes 2097184 | tf_op jit(solution)/shard_map/ppermute | solution.py:14
  143.4 1.8 broadcast_select_fusion.1
  145.2 3.6 collective-permute-done.5
  148.8 1.8 broadcast_select_fusion
  150.6 5.7 %pad_maximum_fusion = bf16[64,128,384]{1,0,2:T(8,128)(2,1)} fusion(bf16[64,128,128]{1,0,2:T(8,128)(2,1)S(1)} %broadcast_select_fusion, bf16[64,128,128]{1,0,2:T(8,128)(2,1)S(1)} %copy.20, bf16[64,128,128]{1,0,2:T(8,128)(2,1)S(1)} %broadcast_select_fusion.1), kind=kLoop, calls=%fused_computation.47 | loop fusion | flops 6291456 | bytes 12582912 | tf_op jit(solution)/shard_map/concatenate | solution.py:88
  156.3 9.8 %gather_fusion = bf16[64,128,128]{1,0,2:T(8,128)(2,1)} fusion(bf16[64,128,384]{1,0,2:T(8,128)(2,1)} %pad_maximum_fusion, s32[64]{0:T(128)S(1)} %get-tuple-element.153), kind=kCustom, calls=%fused_computation | custom fusion | bytes 4195072 | tf_op jit(solution)/shard_map/vmap()/gather | solution.py:25
  166.1 9.8 %gather_fusion.1 = bf16[64,128,128]{1,0,2:T(8,128)(2,1)} fusion(bf16[64,128,384]{1,0,2:T(8,128)(2,1)} %pad_maximum_fusion, s32[64]{0:T(128)S(1)} %get-tuple-element.154), kind=kCustom, calls=%fused_computation.1 | custom fusion | bytes 4195072 | tf_op jit(solution)/shard_map/vmap()/gather | solution.py:27
  175.9 5.2 %add_convert_fusion = bf16[64,128,128]{1,0,2:T(8,128)(2,1)} fusion(bf16[64,128,128]{1,0,2:T(8,128)(2,1)} %gather_fusion.1, bf16[64,128,128]{1,0,2:T(8,128)(2,1)S(1)} %copy.20, bf16[64,128,128]{1,0,2:T(8,128)(2,1)} %gather_fusion, f32[64]{0:T(128)S(1)} %copy-done.5, f32[64]{0:T(128)S(1)} %get-tuple-element.149, f32[64]{0:T(128)S(1)} %get-tuple-element.150, ...), kind=kLoop, calls=%fused_computation.57 | loop fusion | flops 10485760 | bytes 8389632 | tf_op jit(solution)/shard_map/convert_element_type | solution.py:30
  181.1 3.4 copy.24
  184.5 67.5 %while.13 = (s32[]{:T(128)}, f32[4,8,32,64]{2,1,3,0:T(8,128)}, f32[4,8,32,64]{2,1,3,0:T(8,128)}, s32[4]{0:T(128)S(1)}, bf16[128,128]{1,0:T(8,128)(2,1)}, /*index...) while((s32[]{:T(128)}, f32[4,8,32,64]{2,1,3,0:T(8,128)}, ...), condition=%wide.region_4.5_spmd.clone, body=%wide.region_1.4_spmd.clone.sunk | while | flops 399519744 | bytes 14905191 | solution.py:127
  184.8 0.6 dynamic_slice.25
  186.0 1.1 fusion.102
  187.3 1.0 multiply_convert_fusion.2
  188.3 3.1 fusion.103
  191.4 0.2 copy.43
  191.6 0.2 bitcast_add_fusion.2
  191.8 4.9 %fusion.105 = f32[4,8,32,64]{2,1,3,0:T(8,128)} fusion(f32[4,8,32,64]{2,1,3,0:T(8,128)} %get-tuple-element.264, s32[]{:T(128)} %get-tuple-element.262, f32[64,32,128]{2,1,0:T(8,128)S(1)} %bitcast_add_fusion.2, s32[128]{0:T(128)S(1)} %get-tuple-element.293, s32[8]{0:T(128)S(1)} %get-tuple-element.292, s32[8]{0:T(128)S(1)} %get-tuple-element.291), kind=kOutput, calls=%fused_computation.18.clone.1 | convolution fusion | flops 25432064 | bytes 1311808 | tf_op jit(solution)/shard_map/while/body/eval_jaxpr/et,cft->efc/dot_general | solution.py:122
  196.7 4.9 %fusion.104 = f32[4,8,32,64]{2,1,3,0:T(8,128)} fusion(f32[4,8,32,64]{2,1,3,0:T(8,128)} %get-tuple-element.263, s32[]{:T(128)} %get-tuple-element.262, f32[64,32,128]{2,1,0:T(8,128)S(1)} %bitcast_add_fusion.2, s32[128]{0:T(128)S(1)} %get-tuple-element.293, s32[8]{0:T(128)S(1)} %get-tuple-element.292, s32[8]{0:T(128)S(1)} %get-tuple-element.291), kind=kOutput, calls=%fused_computation.20.clone.1 | convolution fusion | flops 25169920 | bytes 1311808 | tf_op jit(solution)/shard_map/while/body/eval_jaxpr/et,cft->efc/dot_general | solution.py:121
  201.6 0.6 dynamic_slice.25
  202.9 1.1 fusion.102
  204.2 1.0 multiply_convert_fusion.2
  205.1 3.1 fusion.103
  208.2 0.2 copy.43
  208.6 4.9 %fusion.105 = f32[4,8,32,64]{2,1,3,0:T(8,128)} fusion(f32[4,8,32,64]{2,1,3,0:T(8,128)} %get-tuple-element.264, s32[]{:T(128)} %get-tuple-element.262, f32[64,32,128]{2,1,0:T(8,128)S(1)} %bitcast_add_fusion.2, s32[128]{0:T(128)S(1)} %get-tuple-element.293, s32[8]{0:T(128)S(1)} %get-tuple-element.292, s32[8]{0:T(128)S(1)} %get-tuple-element.291), kind=kOutput, calls=%fused_computation.18.clone.1 | convolution fusion | flops 25432064 | bytes 1311808 | tf_op jit(solution)/shard_map/while/body/eval_jaxpr/et,cft->efc/dot_general | solution.py:122
  213.5 4.9 %fusion.104 = f32[4,8,32,64]{2,1,3,0:T(8,128)} fusion(f32[4,8,32,64]{2,1,3,0:T(8,128)} %get-tuple-element.263, s32[]{:T(128)} %get-tuple-element.262, f32[64,32,128]{2,1,0:T(8,128)S(1)} %bitcast_add_fusion.2, s32[128]{0:T(128)S(1)} %get-tuple-element.293, s32[8]{0:T(128)S(1)} %get-tuple-element.292, s32[8]{0:T(128)S(1)} %get-tuple-element.291), kind=kOutput, calls=%fused_computation.20.clone.1 | convolution fusion | flops 25169920 | bytes 1311808 | tf_op jit(solution)/shard_map/while/body/eval_jaxpr/et,cft->efc/dot_general | solution.py:121
  218.4 0.6 dynamic_slice.25
  219.7 1.1 fusion.102
  221.0 1.0 multiply_convert_fusion.2
  221.9 3.1 fusion.103
  225.1 0.2 copy.43
  225.3 0.2 bitcast_add_fusion.2
  225.5 4.9 %fusion.105 = f32[4,8,32,64]{2,1,3,0:T(8,128)} fusion(f32[4,8,32,64]{2,1,3,0:T(8,128)} %get-tuple-element.264, s32[]{:T(128)} %get-tuple-element.262, f32[64,32,128]{2,1,0:T(8,128)S(1)} %bitcast_add_fusion.2, s32[128]{0:T(128)S(1)} %get-tuple-element.293, s32[8]{0:T(128)S(1)} %get-tuple-element.292, s32[8]{0:T(128)S(1)} %get-tuple-element.291), kind=kOutput, calls=%fused_computation.18.clone.1 | convolution fusion | flops 25432064 | bytes 1311808 | tf_op jit(solution)/shard_map/while/body/eval_jaxpr/et,cft->efc/dot_general | solution.py:122
  230.4 4.9 %fusion.104 = f32[4,8,32,64]{2,1,3,0:T(8,128)} fusion(f32[4,8,32,64]{2,1,3,0:T(8,128)} %get-tuple-element.263, s32[]{:T(128)} %get-tuple-element.262, f32[64,32,128]{2,1,0:T(8,128)S(1)} %bitcast_add_fusion.2, s32[128]{0:T(128)S(1)} %get-tuple-element.293, s32[8]{0:T(128)S(1)} %get-tuple-element.292, s32[8]{0:T(128)S(1)} %get-tuple-element.291), kind=kOutput, calls=%fused_computation.20.clone.1 | convolution fusion | flops 25169920 | bytes 1311808 | tf_op jit(solution)/shard_map/while/body/eval_jaxpr/et,cft->efc/dot_general | solution.py:121
  235.2 0.6 dynamic_slice.25
  236.5 1.1 fusion.102
  237.8 1.0 multiply_convert_fusion.2
  238.8 3.1 fusion.103
  241.9 0.2 copy.43
  242.3 4.9 %fusion.105 = f32[4,8,32,64]{2,1,3,0:T(8,128)} fusion(f32[4,8,32,64]{2,1,3,0:T(8,128)} %get-tuple-element.264, s32[]{:T(128)} %get-tuple-element.262, f32[64,32,128]{2,1,0:T(8,128)S(1)} %bitcast_add_fusion.2, s32[128]{0:T(128)S(1)} %get-tuple-element.293, s32[8]{0:T(128)S(1)} %get-tuple-element.292, s32[8]{0:T(128)S(1)} %get-tuple-element.291), kind=kOutput, calls=%fused_computation.18.clone.1 | convolution fusion | flops 25432064 | bytes 1311808 | tf_op jit(solution)/shard_map/while/body/eval_jaxpr/et,cft->efc/dot_general | solution.py:122
  247.2 4.9 %fusion.104 = f32[4,8,32,64]{2,1,3,0:T(8,128)} fusion(f32[4,8,32,64]{2,1,3,0:T(8,128)} %get-tuple-element.263, s32[]{:T(128)} %get-tuple-element.262, f32[64,32,128]{2,1,0:T(8,128)S(1)} %bitcast_add_fusion.2, s32[128]{0:T(128)S(1)} %get-tuple-element.293, s32[8]{0:T(128)S(1)} %get-tuple-element.292, s32[8]{0:T(128)S(1)} %get-tuple-element.291), kind=kOutput, calls=%fused_computation.20.clone.1 | convolution fusion | flops 25169920 | bytes 1311808 | tf_op jit(solution)/shard_map/while/body/eval_jaxpr/et,cft->efc/dot_general | solution.py:121
  252.0 1.5 copy.25
  253.6 0.9 reshape.138
  254.5 1.5 copy.26
  256.1 0.9 reshape.139
  257.0 89.1 %reduce-scatter.3.cloned.1.call-done = f32[8,512]{1,0:T(8,128)} async-done(((f32[8,8192]{1,0:T(8,128)}), f32[8,512]{1,0:T(8,128)}) %reduce-scatter.3.cloned.1.call-update) | async-done | bytes 16400 | tf_op jit(solution)/shard_map/reduce_scatter | solution.py:131
  346.1 92.3 %reduce-scatter.5.cloned.1.call-done = f32[8,512]{1,0:T(8,128)} async-done(((f32[8,8192]{1,0:T(8,128)}), f32[8,512]{1,0:T(8,128)}) %reduce-scatter.5.cloned.1.call-update) | async-done | bytes 16400 | tf_op jit(solution)/shard_map/reduce_scatter | solution.py:132
  438.4 1.4 broadcast_divide_fusion
  (76 shorter events, 2.8 us)
Async XLA Ops:
  7.2 9.4 %copy-start = (bf16[64,8,2048]{2,1,0:T(8,128)(2,1)S(1)}, bf16[64,8,2048]{2,1,0:T(8,128)(2,1)}, u32[]{:S(2)}) copy-start(bf16[64,8,2048]{2,1,0:T(8,128)(2,1)} %param.15) | copy-start | bytes 6291460
  7.2 9.4 %copy-start.2 = (bf16[5,64,8]{1,2,0:T(8,128)(2,1)S(1)}, bf16[5,64,8]{1,2,0:T(8,128)(2,1)}, u32[]{:S(2)}) copy-start(bf16[5,64,8]{1,2,0:T(8,128)(2,1)} %param.16) | copy-start | bytes 15364
  7.2 338.9 %reduce-scatter.3.cloned.1.call-start = ((), (), s32[]{:S(2)}) async-start(), calls=%async_computation.3 | async-start | bytes 278528 | tf_op jit(solution)/shard_map/reduce_scatter | solution.py:131
  10.7 10.5 %collective-permute-start = (bf16[64,2,2048]{2,0,1:T(8,128)(2,1)S(1)}, bf16[64,2,2048]{2,0,1:T(8,128)(2,1)S(1)}, u32[]{:S(2)}, u32[]{:S(2)}) collective-permute-start(bf16[64,2,2048]{2,0,1:T(8,128)(2,1)S(1)} %copy.39), channel_id=1, source_target_pairs={{0,32},{32,64},{64,96},{96,128},{128,160},{160,192},{192,224},{224... | collective-permute-start | bytes 1572872 | tf_op jit(solution)/shard_map/ppermute | solution.py:14
  12.8 11.1 %collective-permute-start.1 = (bf16[64,2,2048]{2,0,1:T(8,128)(2,1)S(1)}, bf16[64,2,2048]{2,0,1:T(8,128)(2,1)S(1)}, u32[]{:S(2)}, u32[]{:S(2)}) collective-permute-start(bf16[64,2,2048]{2,0,1:T(8,128)(2,1)S(1)} %copy.38), channel_id=1, source_target_pairs={{32,0},{64,32},{96,64},{128,96},{160,128},{192,160},{224,192},{256... | collective-permute-start | bytes 1572872 | tf_op jit(solution)/shard_map/ppermute | solution.py:17
  23.9 0.7 copy-start.4
  63.9 38.8 %copy-start.11 = (s32[1,8]{1,0:T(1,128)S(1)}, s32[1,8]{1,0:T(1,128)}, u32[]{:S(2)}) copy-start(s32[1,8]{1,0:T(1,128)} %param.27) | copy-start | bytes 100
  63.9 39.0 %copy-start.9 = (s32[64]{0:T(128)S(1)}, s32[64]{0:T(128)}, u32[]{:S(2)}) copy-start(s32[64]{0:T(128)} %param.18) | copy-start | bytes 772
  63.9 39.0 %copy-start.3 = (f32[3,64]{1,0:T(4,128)S(1)}, f32[3,64]{1,0:T(4,128)}, u32[]{:S(2)}) copy-start(f32[3,64]{1,0:T(4,128)} %param.19) | copy-start | bytes 2308
  67.8 28.2 %collective-permute-start.2 = (bf16[64,128,128]{1,0,2:T(8,128)(2,1)S(1)}, bf16[64,128,128]{1,0,2:T(8,128)(2,1)}, u32[]{:S(2)}, u32[]{:S(2)}) collective-permute-start(bf16[64,128,128]{1,0,2:T(8,128)(2,1)S(1)} %copy.20), channel_id=1, source_target_pairs={{0,32},{32,64},{64,96},{96,128},{128,160},{160,192},{192,224},{224... | collective-permute-start | bytes 6291464 | tf_op jit(solution)/shard_map/ppermute | solution.py:14
  70.7 30.4 %collective-permute-start.4 = (bf16[64,128,128]{1,0,2:T(8,128)(2,1)S(1)}, bf16[64,128,128]{1,0,2:T(8,128)(2,1)}, u32[]{:S(2)}, u32[]{:S(2)}) collective-permute-start(bf16[64,128,128]{1,0,2:T(8,128)(2,1)S(1)} %copy.20), channel_id=1, source_target_pairs={{32,0},{64,32},{96,64},{128,96},{160,128},{192,160},{224,192},{256... | collective-permute-start | bytes 6291464 | tf_op jit(solution)/shard_map/ppermute | solution.py:17
  96.0 47.3 %collective-permute-start.3 = (bf16[64,128,128]{1,0,2:T(8,128)(2,1)}, bf16[64,128,128]{1,0,2:T(8,128)(2,1)}, u32[]{:S(2)}, u32[]{:S(2)}) collective-permute-start(bf16[64,128,128]{1,0,2:T(8,128)(2,1)} %collective-permute-done.2), channel_id=1, source_target_pairs={{0,1},{1,2},{2,3},{3,4},{4,5},{5,6},{6,7},{7,8},{8,9},{9,10},{10,1... | collective-permute-start | bytes 6291464 | tf_op jit(solution)/shard_map/ppermute | solution.py:14
  101.2 47.6 %collective-permute-start.5 = (bf16[64,128,128]{1,0,2:T(8,128)(2,1)}, bf16[64,128,128]{1,0,2:T(8,128)(2,1)}, u32[]{:S(2)}, u32[]{:S(2)}) collective-permute-start(bf16[64,128,128]{1,0,2:T(8,128)(2,1)} %collective-permute-done.4), channel_id=1, source_target_pairs={{1,0},{2,1},{3,2},{4,3},{5,4},{6,5},{7,6},{8,7},{9,8},{10,9},{11,1... | collective-permute-start | bytes 6291464 | tf_op jit(solution)/shard_map/ppermute | solution.py:17
  166.1 9.8 %copy-start.5 = (f32[64]{0:T(128)S(1)}, f32[64]{0:T(128)}, u32[]{:S(2)}) copy-start(f32[64]{0:T(128)} %param.20) | copy-start | bytes 772
  181.1 3.4 copy-start.1
  181.1 3.4 copy-start.6
  181.1 3.4 copy-start.7
  181.1 3.4 copy-start.8
  181.1 3.4 copy-start.10
  254.5 183.9 %reduce-scatter.5.cloned.1.call-start = ((), (), s32[]{:S(2)}) async-start(), calls=%async_computation.4 | async-start | bytes 278528 | tf_op jit(solution)/shard_map/reduce_scatter | solution.py:132
Sparse Core Ops, SparseCore 0:
  254.6 91.4 reduce-scatter.2
  350.7 87.6 reduce-scatter.4
